TPU v7x, 32 devices: a whole 2x2x4 slice. The times are simulated.
32 devices in a mesh: row: 8 (over y, x, core), col: 4 (over z).
Axes of the slice: x: 2, y: 2, z: 4, core: 2. Of those that a mesh axis runs over, the one named last changes fastest.
Arguments:
- coeffs: bfloat16 [6144, 4096], P('row', 'col'), may hold values from -0.00390625 to 0.00390625
- occupation: float32 [4096], P('col'), may hold values from 0.5 to 2
- basis_on_grid: bfloat16 [320, 512, 512], P('row'), may hold values from -6 to 6
- basis_map: int32 [320, 512], P('row'), may hold values from 0 to 6143, as said below
- basis_count: int32 [320], P('row'), may hold values from 256 to 512
- batch_atom: int32 [320], P('row'), may hold values from 0 to 63
- harmonics: float32 [320, 49, 512], P('row'), may hold values from -0.25 to 0.25
Outputs:
- density: float32 [320, 512], P('row', 'col')
- moments: float32 [64, 49], replicated
Inputs may be any that keep to these rules, and one draw needn't show every extreme that they name: `basis_map`: the slots of one batch name distinct basis functions. With R = 768 and o = b // 40, batch b names only basis functions q * R + (o * 96 + w) mod R with 0 <= q < 8 and 0 <= w < 96.
All inputs are finite; a program needn't handle non-finite values.
Results may differ from a plain program's by a relative error of at most 0.0003.
Values may be sent and summed in bfloat16 or wider, within the bound.
No kernel may reach another device: no remote copies, remote signals or barrier semaphores. Data moves between devices by JAX's collectives and lax.ppermute only.
A program may use at most 192 MiB of HBM per device.

v0:
```python
import jax
import jax.numpy as jnp
from jax import lax
from jax.sharding import PartitionSpec as P

WIN = 96
NATOM = 64


def shards(coeffs, occupation, basis_on_grid, basis_map, basis_count, batch_atom, harmonics):
    batches, points, slots = basis_on_grid.shape
    owned = coeffs.shape[0]
    owners = lax.axis_size("row")
    target = lax.broadcasted_iota(jnp.int32, (owners, WIN), 0)
    offset = lax.broadcasted_iota(jnp.int32, (owners, WIN), 1)
    outgoing_ids = jnp.mod(target * WIN + offset, owned).reshape(-1)
    outgoing = jnp.take(coeffs, outgoing_ids, axis=0)
    window = lax.all_to_all(outgoing, "row", split_axis=0, concat_axis=0, tiled=True)
    start = jnp.mod(lax.axis_index("row") * WIN, owned)
    source = basis_map // owned
    within = jnp.mod(basis_map % owned - start, owned)
    local_ids = source * WIN + within
    selected = jnp.take(window, local_ids, axis=0)
    slot_ids = lax.broadcasted_iota(jnp.int32, (batches, slots), 1)
    keep = slot_ids < basis_count[:, None]
    masked = jnp.where(keep[:, None, :], basis_on_grid, jnp.zeros_like(basis_on_grid))
    orbital = jnp.einsum("bps,bsk->bpk", masked, selected, preferred_element_type=jnp.float32)
    partial_density = jnp.sum(orbital * orbital * occupation[None, None, :], axis=2)
    atom_ids = lax.broadcasted_iota(jnp.int32, (batches, NATOM), 1)
    member = (batch_atom[:, None] == atom_ids).astype(jnp.float32)
    full_density = lax.psum(partial_density, "col")
    local_moment = jnp.einsum(
        "blp,bp->bl", harmonics, full_density, precision=lax.Precision.HIGHEST
    )
    atom_part = jnp.dot(member.T, local_moment, precision=lax.Precision.HIGHEST)
    moments = lax.psum(atom_part, "row")
    share = points // lax.axis_size("col")
    density = lax.dynamic_slice_in_dim(full_density, lax.axis_index("col") * share, share, 1)
    return (density, moments)


def solution(mesh):
    placed = (
        P("row", "col"),
        P("col"),
        P("row", None, None),
        P("row", None),
        P("row"),
        P("row"),
        P("row", None, None),
    )
    return jax.shard_map(
        shards, mesh=mesh, in_specs=placed, out_specs=(P("row", "col"), P()), check_vma=False
    )
```

profile of v0, /device:TPU:0, one launch (start us, length us, event | category | flops | bytes accessed | tf_op | source)
XLA Modules:
  0.0 228.4 jit_solution(9429908495071229577)
XLA Ops:
  7.2 0.0 copy-start
  7.2 0.1 add_remainder_fusion
  7.3 0.1 compare_and_fusion.1
  7.4 0.1 rem.52
  7.5 1.1 copy-done
  8.6 2.8 %gather_fusion = bf16[768,1024]{1,0:T(8,128)(2,1)S(1)} fusion(bf16[768,1024]{1,0:T(8,128)(2,1)S(1)} %copy-done, s32[1024]{0:T(1024)S(1)} %pad_clamp_fusion), kind=kCustom, calls=%fused_computation | custom fusion | bytes 3148800 | tf_op jit(solution)/shard_map/jit(_take)/gather | solution.py:17
  11.4 1.4 broadcast_select_fusion
  12.8 5.2 %all-to-all-start = ((bf16[8,96,1024]{2,1,0:T(8,128)(2,1)}), bf16[8,96,1024]{2,1,0:T(8,128)(2,1)S(1)}, u32[]{:S(2)}, u32[]{:S(2)}) async-start(bf16[8,96,1024]{2,1,0:T(8,128)(2,1)} %broadcast_select_fusion), calls=%async_computation | async-start | bytes 3145728 | tf_op jit(solution)/shard_map/all_to_all | solution.py:18
  18.0 0.0 all-reduce.2.cloned.1.call-start
  18.0 1.0 compare_and_fusion
  19.1 0.7 iota_compare_fusion
  19.9 19.1 %all-to-all-done = bf16[8,96,1024]{2,1,0:T(8,128)(2,1)S(1)} async-done(((bf16[8,96,1024]{2,1,0:T(8,128)(2,1)}), bf16[8,96,1024]{2,1,0:T(8,128)(2,1)S(1)}, u32[]{:S(2)}, u32[]{:S(2)}) %all-to-all-start) | async-done | bytes 1572896 | tf_op jit(solution)/shard_map/all_to_all | solution.py:18
  39.0 0.0 copy-start.2
  39.0 87.0 %gather_fusion.1 = bf16[20480,1024]{1,0:T(8,128)(2,1)} fusion(bf16[768,1024]{1,0:T(8,128)(2,1)S(1)} %bitcast.9, s32[20480]{0:T(1024)S(1)} %broadcast_clamp_fusion), kind=kCustom, calls=%fused_computation.1 | custom fusion | bytes 83968000 | tf_op jit(solution)/shard_map/jit(_take)/gather | solution.py:23
  125.9 0.0 copy-done.2
  125.9 0.0 copy-start.3
  125.9 0.0 copy-start.1
  125.9 29.3 %multiply_reduce_fusion = f32[40,512]{1,0:T(8,128)} fusion(f32[1024]{0:T(1024)S(1)} %copy-done.2, bf16[40,512,1024]{2,1,0:T(8,128)(2,1)} %bitcast.10, pred[40,512]{1,0:T(8,128)(4,1)S(1)} %get-tuple-element.2, bf16[40,512,512]{2,1,0:T(8,128)(2,1)} %param.9, pred[40,512]{1,0:T(8,128)(4,1)S(1)} %iota_compare_fusion), kind=kOutput, calls=%fused_computation.2 | convolution fusion | flops 21569187840 | bytes 63041536 | tf_op jit(solution)/shard_map/bps,bsk->bpk/dot_general | solution.py:27
  155.2 0.0 all-reduce.2.cloned.1.call-update
  155.3 33.8 %all-reduce.2.cloned.1.call-done = f32[40,512]{1,0:T(8,128)} async-done(((f32[40,512]{1,0:T(8,128)}), f32[40,512]{1,0:T(8,128)}) %all-reduce.2.cloned.1.call-update) | async-done | bytes 81936 | tf_op jit(solution)/shard_map/psum | solution.py:31
  189.0 7.9 %fusion.11 = f32[40,1,49]{2,1,0:T(1,128)S(1)} fusion(f32[40,49,512]{2,0,1:T(8,128)} %param.13, f32[40,512,1]{1,0,2:T(8,128)} %bitcast.14), kind=kOutput, calls=%fused_computation.10 | convolution fusion | flops 12042240 | bytes 4103840 | tf_op jit(solution)/shard_map/blp,bp->bl/dot_general | solution.py:32
  196.9 0.0 copy-done.3
  196.9 0.2 fusion.19
  197.2 23.0 %psum.15 = f32[64,49]{0,1:T(8,128)} all-reduce(f32[64,49]{0,1:T(8,128)S(1)} %fusion.19), channel_id=1, replica_groups=mesh['row'=8,'col'=4] {'row'}, use_global_device_ids=true, to_apply=%region_2.3 | all-reduce | flops 3136 | bytes 25088 | tf_op jit(solution)/shard_map/psum | solution.py:36
  220.2 1.3 constant_dynamic-slice_fusion
  221.5 0.0 copy-done.1
  (5 shorter events, 0.1 us)
Async XLA Ops:
  7.2 1.4 copy-start
  12.8 26.2 %all-to-all-start = ((bf16[8,96,1024]{2,1,0:T(8,128)(2,1)}), bf16[8,96,1024]{2,1,0:T(8,128)(2,1)S(1)}, u32[]{:S(2)}, u32[]{:S(2)}) async-start(bf16[8,96,1024]{2,1,0:T(8,128)(2,1)} %broadcast_select_fusion), calls=%async_computation | async-start | bytes 3145728 | tf_op jit(solution)/shard_map/all_to_all | solution.py:18
  18.0 171.1 %all-reduce.2.cloned.1.call-start = ((), (), s32[]{:S(2)}) async-start(), calls=%async_computation.1 | async-start | bytes 163840 | tf_op jit(solution)/shard_map/psum | solution.py:31
  39.0 87.0 %copy-start.2 = (f32[1024]{0:T(1024)S(1)}, f32[1024]{0:T(1024)}, u32[]{:S(2)}) copy-start(f32[1024]{0:T(1024)} %param.8) | copy-start | bytes 12292
  125.9 71.0 %copy-start.3 = (s32[40]{0:T(128)S(1)}, s32[40]{0:T(128)}, u32[]{:S(2)}) copy-start(s32[40]{0:T(128)} %param.12) | copy-start | bytes 484
  125.9 95.6 %copy-start.1 = (bf16[768,1024]{1,0:T(8,128)(2,1)S(1)}, bf16[768,1024]{1,0:T(8,128)(2,1)}, u32[]{:S(2)}) copy-start(bf16[768,1024]{1,0:T(8,128)(2,1)} %param.7) | copy-start | bytes 4718596
Sparse Core Ops, SparseCore 0:
  155.4 33.6 all-reduce.1
where the time goes:
time: 229 us; the launch traced here: 228 us
  local copies, waits for them, and re-layouts  92.3 us (40%)
  waiting for transfers between devices  52.9 us (23%)
  matrix products  37.5 us (16%)
  blocking collectives  23 us (10%)
  between operations  14.1 us (6%)
  starting transfers between devices  5.24 us (2%)
  other arithmetic  3.37 us (1%)
    gather x1, local copies, waits for them, and re-layouts, shards(): selected = jnp.take(window, local_ids, axis=0)  87 us
    psum x1, waiting for transfers between devices, shards(): full_density = lax.psum(partial_density, 'col')  33.8 us
    dot_general x1, matrix products, shards(): jnp.einsum('bps,bsk->bpk', masked, selected, preferred_element_type=jnp.f...  29.3 us
    psum x1, blocking collectives, shards(): moments = lax.psum(atom_part, 'row')  23 us
    all_to_all x1, waiting for transfers between devices, shards(): lax.all_to_all(outgoing, 'row', split_axis=0, concat_axis=0, tiled=True)  19.1 us
    dot_general x1, matrix products, shards(): jnp.einsum('blp,bp->bl', harmonics, full_density, precision=lax.Precision...  7.89 us
    all_to_all x1, starting transfers between devices, shards(): lax.all_to_all(outgoing, 'row', split_axis=0, concat_axis=0, tiled=True)  5.2 us
  transfers between devices with their start and end apart: 2, of which 2 were waited for; matrix products, arithmetic and copies ran while one was open for 1% of the time, Pallas kernels for 0%

commit v1 on v0

--- a/solution.py
+++ b/solution.py
@@ -28,7 +28,7 @@
     partial_density = jnp.sum(orbital * orbital * occupation[None, None, :], axis=2)
     atom_ids = lax.broadcasted_iota(jnp.int32, (batches, NATOM), 1)
     member = (batch_atom[:, None] == atom_ids).astype(jnp.float32)
-    full_density = lax.psum(partial_density, "col")
+    full_density = jnp.sum(lax.all_gather(partial_density, "col"), 0)
     local_moment = jnp.einsum(
         "blp,bp->bl", harmonics, full_density, precision=lax.Precision.HIGHEST
     )

time: 229 us -> 195 us (0.85)
  waiting for transfers between devices: 52.9 us -> 19.1 us
  blocking collectives: 23 us -> 38 us
  between operations: 14.1 us -> 0.72 us
    psum x1 -> x0, waiting for transfers between devices: 33.8 us -> none  [shards(): full_density = lax.psum(partial_density, 'col')]
    all_gather x0 -> x1, blocking collectives: none -> 15 us  [shards(): full_density = jnp.sum(lax.all_gather(partial_density, 'col'), 0)]
  transfers between devices with their start and end apart: 2 -> 1, of which waited for: 2 -> 1; matrix products, arithmetic and copies ran while one was open for 1% -> 1% of each run, Pallas kernels for 0% -> 0%
where the time goes in v1:
time: 195 us
  local copies, waits for them, and re-layouts  91.6 us (47%)
  blocking collectives  38 us (19%)
  matrix products  36.8 us (19%)
  waiting for transfers between devices  19.1 us (10%)
  starting transfers between devices  5.2 us (3%)
  other arithmetic  3.39 us (2%)
    gather x1, local copies, waits for them, and re-layouts, shards(): selected = jnp.take(window, local_ids, axis=0)  87 us
    dot_general x1, matrix products, shards(): jnp.einsum('bps,bsk->bpk', masked, selected, preferred_element_type=jnp.f...  28.7 us
    psum x1, blocking collectives, shards(): moments = lax.psum(atom_part, 'row')  23 us
    all_to_all x1, waiting for transfers between devices, shards(): lax.all_to_all(outgoing, 'row', split_axis=0, concat_axis=0, tiled=True)  19.1 us
    all_gather x1, blocking collectives, shards(): full_density = jnp.sum(lax.all_gather(partial_density, 'col'), 0)  15 us
    dot_general x1, matrix products, shards(): jnp.einsum('blp,bp->bl', harmonics, full_density, precision=lax.Precision...  7.84 us
    all_to_all x1, starting transfers between devices, shards(): lax.all_to_all(outgoing, 'row', split_axis=0, concat_axis=0, tiled=True)  5.2 us
  transfers between devices with their start and end apart: 1, of which 1 were waited for; matrix products, arithmetic and copies ran while one was open for 1% of the time, Pallas kernels for 0%

profile of v1, /device:TPU:0, one launch (start us, length us, event | category | flops | bytes accessed | tf_op | source)
XLA Modules:
  0.0 194.8 jit_solution(12261363362341990561)
XLA Ops:
  0.6 0.0 copy-start
  0.7 0.1 add_remainder_fusion
  0.7 0.1 compare_and_fusion.1
  0.8 0.1 rem.52
  0.9 1.1 copy-done
  2.0 2.8 %gather_fusion = bf16[768,1024]{1,0:T(8,128)(2,1)S(1)} fusion(bf16[768,1024]{1,0:T(8,128)(2,1)S(1)} %copy-done, s32[1024]{0:T(1024)S(1)} %pad_clamp_fusion), kind=kCustom, calls=%fused_computation | custom fusion | bytes 3148800 | tf_op jit(solution)/shard_map/jit(_take)/gather | solution.py:17
  4.9 1.4 broadcast_select_fusion
  6.2 5.2 %all-to-all-start = ((bf16[8,96,1024]{2,1,0:T(8,128)(2,1)}), bf16[8,96,1024]{2,1,0:T(8,128)(2,1)S(1)}, u32[]{:S(2)}, u32[]{:S(2)}) async-start(bf16[8,96,1024]{2,1,0:T(8,128)(2,1)} %broadcast_select_fusion), calls=%async_computation | async-start | bytes 3145728 | tf_op jit(solution)/shard_map/all_to_all | solution.py:18
  11.4 1.0 compare_and_fusion
  12.5 0.7 iota_compare_fusion
  13.3 19.1 %all-to-all-done = bf16[8,96,1024]{2,1,0:T(8,128)(2,1)S(1)} async-done(((bf16[8,96,1024]{2,1,0:T(8,128)(2,1)}), bf16[8,96,1024]{2,1,0:T(8,128)(2,1)S(1)}, u32[]{:S(2)}, u32[]{:S(2)}) %all-to-all-start) | async-done | bytes 1572896 | tf_op jit(solution)/shard_map/all_to_all | solution.py:18
  32.4 0.0 copy-start.2
  32.4 87.0 %gather_fusion.1 = bf16[20480,1024]{1,0:T(8,128)(2,1)} fusion(bf16[768,1024]{1,0:T(8,128)(2,1)S(1)} %bitcast.10, s32[20480]{0:T(1024)S(1)} %broadcast_clamp_fusion), kind=kCustom, calls=%fused_computation.1 | custom fusion | bytes 83968000 | tf_op jit(solution)/shard_map/jit(_take)/gather | solution.py:23
  119.4 0.0 copy-done.2
  119.4 0.0 copy-start.3
  119.4 0.0 copy-start.1
  119.4 28.7 %multiply_reduce_fusion = f32[40,512]{1,0:T(8,128)S(1)} fusion(f32[1024]{0:T(1024)S(1)} %copy-done.2, bf16[40,512,1024]{2,1,0:T(8,128)(2,1)} %bitcast.11, pred[40,512]{1,0:T(8,128)(4,1)S(1)} %get-tuple-element.2, bf16[40,512,512]{2,1,0:T(8,128)(2,1)} %param.9, pred[40,512]{1,0:T(8,128)(4,1)S(1)} %iota_compare_fusion), kind=kOutput, calls=%fused_computation.2 | convolution fusion | flops 21569187840 | bytes 63041536 | tf_op jit(solution)/shard_map/bps,bsk->bpk/dot_general | solution.py:27
  148.1 15.0 %all-gather = f32[160,512]{1,0:T(8,128)S(1)} all-gather(f32[40,512]{1,0:T(8,128)S(1)} %multiply_reduce_fusion), channel_id=2, replica_groups=mesh['row'=8,'col'=4] {'col'}, dimensions={0}, use_global_device_ids=true | all-gather | bytes 409600 | tf_op jit(solution)/shard_map/all_gather | solution.py:31
  163.1 0.6 constant_dynamic-slice_fusion
  163.8 7.8 %fusion.11 = f32[40,1,49]{2,1,0:T(1,128)S(1)} fusion(f32[40,49,512]{2,0,1:T(8,128)} %param.13, f32[40,512,1]{1,0,2:T(8,128)S(1)} %bitcast.14), kind=kOutput, calls=%fused_computation.10 | convolution fusion | flops 12042240 | bytes 4103840 | tf_op jit(solution)/shard_map/blp,bp->bl/dot_general | solution.py:32
  171.6 0.0 copy-done.3
  171.6 0.2 fusion.19
  171.8 23.0 %psum.7 = f32[64,49]{0,1:T(8,128)} all-reduce(f32[64,49]{0,1:T(8,128)S(1)} %fusion.19), channel_id=1, replica_groups=mesh['row'=8,'col'=4] {'row'}, use_global_device_ids=true, to_apply=%region_2.3 | all-reduce | flops 3136 | bytes 25088 | tf_op jit(solution)/shard_map/psum | solution.py:36
  194.8 0.0 copy-done.1
  (6 shorter events, 0.1 us)
Async XLA Ops:
  0.6 1.4 copy-start
  6.2 26.2 %all-to-all-start = ((bf16[8,96,1024]{2,1,0:T(8,128)(2,1)}), bf16[8,96,1024]{2,1,0:T(8,128)(2,1)S(1)}, u32[]{:S(2)}, u32[]{:S(2)}) async-start(bf16[8,96,1024]{2,1,0:T(8,128)(2,1)} %broadcast_select_fusion), calls=%async_computation | async-start | bytes 3145728 | tf_op jit(solution)/shard_map/all_to_all | solution.py:18
  32.4 87.0 %copy-start.2 = (f32[1024]{0:T(1024)S(1)}, f32[1024]{0:T(1024)}, u32[]{:S(2)}) copy-start(f32[1024]{0:T(1024)} %param.8) | copy-start | bytes 12292
  119.4 52.2 %copy-start.3 = (s32[40]{0:T(128)S(1)}, s32[40]{0:T(128)}, u32[]{:S(2)}) copy-start(s32[40]{0:T(128)} %param.12) | copy-start | bytes 484
  119.4 75.5 %copy-start.1 = (bf16[768,1024]{1,0:T(8,128)(2,1)S(1)}, bf16[768,1024]{1,0:T(8,128)(2,1)}, u32[]{:S(2)}) copy-start(bf16[768,1024]{1,0:T(8,128)(2,1)} %param.7) | copy-start | bytes 4718596
